TPU v7x, 512 devices: a whole 4x8x8 slice. The times are simulated.
512 devices in a mesh: tm: 32 (over z, x), frac: 16 (over y, core).
Axes of the slice: x: 4, y: 8, z: 8, core: 2. Of those that a mesh axis runs over, the one named last changes fastest.
Arguments:
- pressure0: float32 [64, 32, 128], P('frac'), may hold values from -6 to 6
- storage: float32 [64, 32, 128], P('frac'), may hold values from 0.1 to 1
- perm_base: float32 [64, 32, 128], P('frac'), may hold values from 0.2 to 5
- leakoff: float32 [64, 32, 128], P('frac'), may hold values from 0.5 to 2
- sources: float32 [32, 64, 32, 128], P('tm', 'frac'), may hold values from -6 to 6
- export_cells: int32 [4096], P('frac'), may hold values from 0 to 16383
- inter_local: int32 [16384], P('frac'), may hold values from 0 to 16383
- trace_source: int32 [16384], P('frac'), may hold values from 0 to 4095, as said below
- inter_trans: float32 [16384], P('frac'), may hold values from 0.5 to 4
- inter_count: int32 [16], P('frac'), may hold values from 1 to 1024, 8192 in all
Outputs:
- slice_pressure: float32 [32, 64, 32, 128], P('tm', 'frac')
Inputs may be any that keep to these rules, and one draw needn't show every extreme that they name: An entry of frac index d names a slot of another frac index: trace_source // 256 differs from d. `inter_count`: the live entries of a frac index are its first ones; the largest count is 1024.
All inputs are finite; a program needn't handle non-finite values. No bound on the sum of `inter_count` on one device may be relied on, other than what follows from the above.
Results may differ from a plain program's by a relative error of at most 0.00002.
Values sent between devices are 32-bit elements; how exact they have to be, the bound alone decides.
A program may use at most 64 MiB of HBM per device.

v0:
```python
import jax
import jax.numpy as jnp
from jax import lax
from jax.sharding import PartitionSpec as P

FINE_STEPS = 4
SWEEPS = 8
COARSE_SWEEPS = 2
ITERS = 2
stress_factor = 0.15
fine_size = 0.25


def next_rows(array):
    return jnp.concatenate([array[:, 1:, :], jnp.zeros_like(array[:, :1, :])], axis=1)


def prev_rows(array):
    return jnp.concatenate([jnp.zeros_like(array[:, :1, :]), array[:, :-1, :]], axis=1)


def next_cols(array):
    return jnp.concatenate([array[:, :, 1:], jnp.zeros_like(array[:, :, :1])], axis=2)


def prev_cols(array):
    return jnp.concatenate([jnp.zeros_like(array[:, :, :1]), array[:, :, :-1]], axis=2)


def implicit(pressure, slice_source, step_size, sweeps, fields, couple):
    storage, perm_base, leakoff, tisum = fields
    permeability = perm_base * jnp.exp(stress_factor * pressure)
    row_index = lax.broadcasted_iota(jnp.int32, pressure.shape, 1)
    col_index = lax.broadcasted_iota(jnp.int32, pressure.shape, 2)
    face_rows = jnp.where(
        row_index < pressure.shape[1] - 1, 0.5 * (permeability + next_rows(permeability)), 0.0
    )
    face_cols = jnp.where(
        col_index < pressure.shape[2] - 1, 0.5 * (permeability + next_cols(permeability)), 0.0
    )
    storage_rate = storage / step_size
    diagonal_total = (
        storage_rate + leakoff + face_rows + prev_rows(face_rows) + face_cols + prev_cols(face_cols)
    )
    right_side = storage_rate * pressure + slice_source
    if couple is not None:
        diagonal_total = diagonal_total + tisum
        right_side = right_side + couple(pressure)

    def sweep(sweep_index, current):
        beside = face_rows * next_rows(current) + prev_rows(face_rows * current)
        beside = beside + face_cols * next_cols(current) + prev_cols(face_cols * current)
        return (right_side + beside) / diagonal_total

    return lax.fori_loop(0, sweeps, sweep, pressure)


def body(
    pressure0,
    storage,
    perm_base,
    leakoff,
    sources,
    export_cells,
    inter_local,
    trace_source,
    inter_trans,
    inter_count,
):
    slice_count = lax.axis_size("tm")
    slice_index = lax.axis_index("tm")
    own_source = sources[0]
    entry_index = lax.broadcasted_iota(jnp.int32, inter_local.shape, 0)
    weights = jnp.where(entry_index < inter_count[0], inter_trans, jnp.zeros_like(inter_trans))
    cell_total = pressure0.size
    tisum = (
        jnp.zeros((cell_total,), jnp.float32).at[inter_local].add(weights).reshape(pressure0.shape)
    )
    fields = (storage, perm_base, leakoff, tisum)

    def couple(current):
        flat_field = current.reshape(-1)
        exported = flat_field[export_cells]
        gathered = lax.all_gather(exported, "frac", axis=0, tiled=True)
        remote_values = gathered[trace_source]
        return (
            jnp.zeros_like(flat_field)
            .at[inter_local]
            .add(weights * remote_values)
            .reshape(current.shape)
        )

    def coarse(pressure, slice_source):
        return implicit(pressure, slice_source, fine_size * FINE_STEPS, COARSE_SWEEPS, fields, None)

    all_sources = lax.all_gather(sources, "tm", axis=0, tiled=True)

    def chain(correction, carry_zero):
        if carry_zero:
            all_corrections = jnp.zeros_like(all_sources)
        else:
            all_corrections = lax.all_gather(correction[None], "tm", axis=0, tiled=True)

        def turn(turn_index, carried):
            current, kept_state = carried
            slice_source = lax.dynamic_index_in_dim(all_sources, turn_index, 0, keepdims=False)
            added = lax.dynamic_index_in_dim(all_corrections, turn_index, 0, keepdims=False)
            current = coarse(current, slice_source) + added
            kept_state = jnp.where(slice_index == turn_index + 1, current, kept_state)
            return (current, kept_state)

        final_pair = lax.fori_loop(0, slice_count - 1, turn, (pressure0, pressure0))
        return final_pair[1]

    state = chain(jnp.zeros_like(pressure0), True)
    for iteration in range(ITERS):
        fine_pressure = state
        for step_number in range(FINE_STEPS):
            fine_pressure = implicit(fine_pressure, own_source, fine_size, SWEEPS, fields, couple)
        coarse_end = coarse(state, own_source)
        state = chain(fine_pressure - coarse_end, False)
    return state[None]


def solution(mesh):
    placed = (
        P("frac", None, None),
        P("frac", None, None),
        P("frac", None, None),
        P("frac", None, None),
        P("tm", "frac", None, None),
        P("frac"),
        P("frac"),
        P("frac"),
        P("frac"),
        P("frac"),
    )
    return jax.shard_map(
        body, mesh=mesh, in_specs=placed, out_specs=P("tm", "frac", None, None), check_vma=False
    )
```

profile of v0, /device:TPU:8, one launch (start us, length us, event | category | flops | bytes accessed | tf_op | source)
XLA Modules:
  0.0 733.0 jit_solution(9327614761849319025)
XLA Ops:
  11.1 88.0 %all-gather.22.cloned.1.call-done = f32[32,4,32,128]{3,2,1,0:T(8,128)} async-done(((f32[1,4,32,128]{3,2,1,0:T(8,128)}), f32[32,4,32,128]{3,2,1,0:T(8,128)}) %all-gather.22.cloned.1.call-update) | async-done | bytes 2097168 | tf_op jit(solution)/shard_map/all_gather | solution.py:96
  99.1 52.9 %while.235 = (s32[]{:T(128)}, f32[4,32,128]{2,1,0:T(8,128)S(1)}, f32[4,32,128]{2,1,0:T(8,128)S(1)}, f32[4,32,128]{2,1,0:T(8,128)}, f32[4,32,128]{2,1,0:T(8,128)}...) while((s32[]{:T(128)}, f32[4,32,128]{2,1,0:T(8,128)S(1)}, ...), condition=%wide.region_3.4_spmd, body=%wide.region_0.3_spmd.sunk | while | flops 392741 | bytes 2790472 | solution.py:112
  154.8 15.7 %all-gather.10 = f32[16,1,256]{2,1,0:T(1,128)S(1)} all-gather(f32[1,1,256]{2,1,0:T(1,128)S(1)} %bitcast.174), channel_id=2, replica_groups=mesh['tm'=32,'frac'=16] {'frac'}, dimensions={0}, use_global_device_ids=true | all-gather | bytes 17408 | tf_op jit(solution)/shard_map/all_gather | solution.py:84
  170.5 6.1 gather_fusion.1
  182.6 5.9 scatter_custom_fusion
  192.2 16.0 %all-gather.11 = f32[16,1,256]{2,1,0:T(1,128)S(1)} all-gather(f32[1,1,256]{2,1,0:T(1,128)S(1)} %bitcast.175), channel_id=3, replica_groups=mesh['tm'=32,'frac'=16] {'frac'}, dimensions={0}, use_global_device_ids=true | all-gather | bytes 17408 | tf_op jit(solution)/shard_map/all_gather | solution.py:84
  208.2 6.1 gather_fusion.3
  224.1 15.2 %all-gather.12 = f32[16,1,256]{2,1,0:T(1,128)S(1)} all-gather(f32[1,1,256]{2,1,0:T(1,128)S(1)} %bitcast.176), channel_id=4, replica_groups=mesh['tm'=32,'frac'=16] {'frac'}, dimensions={0}, use_global_device_ids=true | all-gather | bytes 17408 | tf_op jit(solution)/shard_map/all_gather | solution.py:84
  239.3 6.1 gather_fusion.5
  245.5 5.9 scatter_custom_fusion.3
  255.2 15.1 %all-gather.13 = f32[16,1,256]{2,1,0:T(1,128)S(1)} all-gather(f32[1,1,256]{2,1,0:T(1,128)S(1)} %bitcast.177), channel_id=5, replica_groups=mesh['tm'=32,'frac'=16] {'frac'}, dimensions={0}, use_global_device_ids=true | all-gather | bytes 17408 | tf_op jit(solution)/shard_map/all_gather | solution.py:84
  270.3 6.1 gather_fusion.7
  285.8 79.1 %all-gather.24.cloned.1.call-done = f32[128,32,128]{2,1,0:T(8,128)} async-done(((f32[4,32,128]{2,1,0:T(8,128)}), f32[128,32,128]{2,1,0:T(8,128)}) %all-gather.24.cloned.1.call-update) | async-done | bytes 2097168 | tf_op jit(solution)/shard_map/all_gather | solution.py:102
  364.9 77.4 %while.242 = (s32[]{:T(128)}, f32[4,32,128]{2,1,0:T(8,128)S(1)}, f32[4,32,128]{2,1,0:T(8,128)S(1)}, f32[4,32,128]{2,1,0:T(8,128)S(1)}, f32[4,32,128]{2,1,0:T(8,1...) while((s32[]{:T(128)}, f32[4,32,128]{2,1,0:T(8,128)S(1)}, ...), condition=%wide.region_22.23_spmd, body=%wide.region_19.22_spmd.sunk | while | flops 409125 | bytes 2921564 | solution.py:112
  444.1 15.7 %all-gather.14 = f32[16,1,256]{2,1,0:T(1,128)S(1)} all-gather(f32[1,1,256]{2,1,0:T(1,128)S(1)} %bitcast.178), channel_id=7, replica_groups=mesh['tm'=32,'frac'=16] {'frac'}, dimensions={0}, use_global_device_ids=true | all-gather | bytes 17408 | tf_op jit(solution)/shard_map/all_gather | solution.py:84
  459.8 6.1 gather_fusion.9
  475.7 16.0 %all-gather.15 = f32[16,1,256]{2,1,0:T(1,128)S(1)} all-gather(f32[1,1,256]{2,1,0:T(1,128)S(1)} %bitcast.179), channel_id=8, replica_groups=mesh['tm'=32,'frac'=16] {'frac'}, dimensions={0}, use_global_device_ids=true | all-gather | bytes 17408 | tf_op jit(solution)/shard_map/all_gather | solution.py:84
  491.7 6.1 gather_fusion.11
  507.6 15.2 %all-gather.16 = f32[16,1,256]{2,1,0:T(1,128)S(1)} all-gather(f32[1,1,256]{2,1,0:T(1,128)S(1)} %bitcast.180), channel_id=9, replica_groups=mesh['tm'=32,'frac'=16] {'frac'}, dimensions={0}, use_global_device_ids=true | all-gather | bytes 17408 | tf_op jit(solution)/shard_map/all_gather | solution.py:84
  522.8 6.1 gather_fusion.13
  538.7 15.1 %all-gather.17 = f32[16,1,256]{2,1,0:T(1,128)S(1)} all-gather(f32[1,1,256]{2,1,0:T(1,128)S(1)} %bitcast.173), channel_id=10, replica_groups=mesh['tm'=32,'frac'=16] {'frac'}, dimensions={0}, use_global_device_ids=true | all-gather | bytes 17408 | tf_op jit(solution)/shard_map/all_gather | solution.py:84
  553.8 6.1 gather_fusion.15
  569.0 79.4 %all-gather.26.cloned.1.call-done = f32[128,32,128]{2,1,0:T(8,128)} async-done(((f32[4,32,128]{2,1,0:T(8,128)}), f32[128,32,128]{2,1,0:T(8,128)}) %all-gather.26.cloned.1.call-update) | async-done | bytes 2097168 | tf_op jit(solution)/shard_map/all_gather | solution.py:102
  648.4 77.4 %while.249 = (s32[]{:T(128)}, f32[4,32,128]{2,1,0:T(8,128)S(1)}, f32[4,32,128]{2,1,0:T(8,128)S(1)}, f32[4,32,128]{2,1,0:T(8,128)S(1)}, f32[4,32,128]{2,1,0:T(8,1...) while((s32[]{:T(128)}, f32[4,32,128]{2,1,0:T(8,128)S(1)}, ...), condition=%wide.region_40.41_spmd, body=%wide.region_37.40_spmd.sunk | while | flops 409125 | bytes 2921564 | solution.py:112
  (1707 shorter events, 330.9 us)
Async XLA Ops:
  6.5 92.6 %all-gather.22.cloned.1.call-start = ((), (), s32[]{:S(2)}) async-start(), calls=%async_computation | async-start | bytes 2162688 | tf_op jit(solution)/shard_map/all_gather | solution.py:96
  7.4 357.5 %all-gather.24.cloned.1.call-start = ((), (), s32[]{:S(2)}) async-start(), calls=%async_computation.1 | async-start | bytes 2162688 | tf_op jit(solution)/shard_map/all_gather | solution.py:102
  170.5 6.2 copy-start.5
  170.5 18.2 %copy-start = (f32[4,32,128]{2,1,0:T(8,128)S(1)}, f32[4,32,128]{2,1,0:T(8,128)}, u32[]{:S(2)}) copy-start(f32[4,32,128]{2,1,0:T(8,128)} %get-tuple-element.2573) | copy-start | bytes 196612
  170.5 18.2 %copy-start.2 = (f32[1,4,32,128]{3,2,1,0:T(8,128)S(1)}, f32[1,4,32,128]{3,2,1,0:T(8,128)}, u32[]{:S(2)}) copy-start(f32[1,4,32,128]{3,2,1,0:T(8,128)} %param.46) | copy-start | bytes 196612
  170.5 18.2 %copy-start.4 = (f32[4,32,128]{2,1,0:T(8,128)S(1)}, f32[4,32,128]{2,1,0:T(8,128)}, u32[]{:S(2)}) copy-start(f32[4,32,128]{2,1,0:T(8,128)} %param.45) | copy-start | bytes 196612
  208.2 12.1 %copy-start.1 = (f32[4,32,128]{2,1,0:T(8,128)S(1)}, f32[4,32,128]{2,1,0:T(8,128)}, u32[]{:S(2)}) copy-start(f32[4,32,128]{2,1,0:T(8,128)} %get-tuple-element.2579) | copy-start | bytes 196612
  285.5 362.8 %all-gather.26.cloned.1.call-start = ((), (), s32[]{:S(2)}) async-start(), calls=%async_computation.2 | async-start | bytes 2162688 | tf_op jit(solution)/shard_map/all_gather | solution.py:102
  725.8 0.6 copy-start.3
Sparse Core Ops, SparseCore 0:
  10.5 88.6 all-gather.21
  285.7 79.2 all-gather.23
  569.1 79.2 all-gather.25
where the time goes:
time: 741 us; the launch traced here: 733 us
  other arithmetic  264 us (36%)
  waiting for transfers between devices  247 us (33%)
  blocking collectives  124 us (17%)
  local copies, waits for them, and re-layouts  73.4 us (10%)
  between operations  14.4 us (2%)
  loops' own time  10.6 us (1%)
    all_gather x2, waiting for transfers between devices, chain(): all_corrections = lax.all_gather(correction[None], 'tm', axis=0, tiled=True)  159 us
    all_gather x8, blocking collectives, couple(): gathered = lax.all_gather(exported, 'frac', axis=0, tiled=True)  124 us
    all_gather x1, waiting for transfers between devices, body(): all_sources = lax.all_gather(sources, 'tm', axis=0, tiled=True)  88 us
    add x94, other arithmetic, implicit(): right_side = storage_rate * pressure + slice_source  82.8 us
    select_n x93, other arithmetic, turn(): kept_state = jnp.where(slice_index == turn_index + 1, current, kept_state)  55 us
    gather x8, local copies, waits for them, and re-layouts, couple(): remote_values = gathered[trace_source]  49.2 us
    scatter-add x8, other arithmetic, couple(): return jnp.zeros_like(flat_field).at[inter_local].add(weights * remote_va...  47.6 us
    div x254, other arithmetic, sweep(): return (right_side + beside) / diagonal_total  25 us
  transfers between devices with their start and end apart: 3, of which 3 were waited for; matrix products, arithmetic and copies ran while one was open for 0% of the time, Pallas kernels for 0%

commit v1 on v0

--- a/solution.py
+++ b/solution.py
@@ -99,7 +99,11 @@
         if carry_zero:
             all_corrections = jnp.zeros_like(all_sources)
         else:
-            all_corrections = lax.all_gather(correction[None], "tm", axis=0, tiled=True)
+            count = lax.axis_size("tm")
+            repeats = [count if d == 0 else 1 for d in range(correction[None].ndim)]
+            all_corrections = lax.all_to_all(
+                jnp.tile(correction[None], repeats), "tm", split_axis=0, concat_axis=0, tiled=True
+            )
 
         def turn(turn_index, carried):
             current, kept_state = carried

time: 741 us -> 640 us (0.86)
  the two profiles are of different devices: /device:TPU:8 before, /device:TPU:5 now
where the time goes in v1:
time: 640 us; the launch traced here: 635 us
  other arithmetic  210 us (33%)
  waiting for transfers between devices  182 us (28%)
  blocking collectives  128 us (20%)
  local copies, waits for them, and re-layouts  76.7 us (12%)
  between operations  14.7 us (2%)
  starting transfers between devices  12.3 us (2%)
  loops' own time  10.8 us (2%)
    all_gather x8, blocking collectives, couple(): gathered = lax.all_gather(exported, 'frac', axis=0, tiled=True)  128 us
    all_to_all x2, waiting for transfers between devices, chain(): lax.all_to_all(jnp.tile(correction[None], repeats), 'tm', split_axis=0, c...  99.9 us
    add x94, other arithmetic, implicit(): right_side = storage_rate * pressure + slice_source  82.8 us
    all_gather x1, waiting for transfers between devices, body(): all_sources = lax.all_gather(sources, 'tm', axis=0, tiled=True)  82.3 us
    gather x8, local copies, waits for them, and re-layouts, couple(): remote_values = gathered[trace_source]  49.2 us
    scatter-add x8, other arithmetic, couple(): return jnp.zeros_like(flat_field).at[inter_local].add(weights * remote_va...  47.6 us
    div x254, other arithmetic, sweep(): return (right_side + beside) / diagonal_total  25 us
    slice x254, other arithmetic, next_cols(): array[:, :, 1:]  20.6 us
  transfers between devices with their start and end apart: 3, of which 3 were waited for; matrix products, arithmetic and copies ran while one was open for 0% of the time, Pallas kernels for 0%

profile of v1, /device:TPU:5, one launch (start us, length us, event | category | flops | bytes accessed | tf_op | source)
XLA Modules:
  0.0 634.8 jit_solution(13973755785336166617)
XLA Ops:
  11.1 82.3 %all-gather.18.cloned.1.call-done = f32[32,4,32,128]{3,2,1,0:T(8,128)} async-done(((f32[1,4,32,128]{3,2,1,0:T(8,128)}), f32[32,4,32,128]{3,2,1,0:T(8,128)}) %all-gather.18.cloned.1.call-update) | async-done | bytes 2097168 | tf_op jit(solution)/shard_map/all_gather | solution.py:96
  93.4 52.9 %while.235 = (s32[]{:T(128)}, f32[4,32,128]{2,1,0:T(8,128)S(1)}, f32[4,32,128]{2,1,0:T(8,128)S(1)}, f32[4,32,128]{2,1,0:T(8,128)}, f32[4,32,128]{2,1,0:T(8,128)}...) while((s32[]{:T(128)}, f32[4,32,128]{2,1,0:T(8,128)S(1)}, ...), condition=%wide.region_3.4_spmd, body=%wide.region_0.3_spmd.sunk | while | flops 392741 | bytes 2790472 | solution.py:116
  149.0 21.9 %all-gather.8 = f32[16,1,256]{2,1,0:T(1,128)S(1)} all-gather(f32[1,1,256]{2,1,0:T(1,128)S(1)} %bitcast.170), channel_id=2, replica_groups=mesh['tm'=32,'frac'=16] {'frac'}, dimensions={0}, use_global_device_ids=true | all-gather | bytes 17408 | tf_op jit(solution)/shard_map/all_gather | solution.py:84
  170.9 6.2 gather_fusion.1
  192.7 15.2 %all-gather.9 = f32[16,1,256]{2,1,0:T(1,128)S(1)} all-gather(f32[1,1,256]{2,1,0:T(1,128)S(1)} %bitcast.171), channel_id=3, replica_groups=mesh['tm'=32,'frac'=16] {'frac'}, dimensions={0}, use_global_device_ids=true | all-gather | bytes 17408 | tf_op jit(solution)/shard_map/all_gather | solution.py:84
  207.9 6.1 gather_fusion.3
  223.8 15.1 %all-gather.10 = f32[16,1,256]{2,1,0:T(1,128)S(1)} all-gather(f32[1,1,256]{2,1,0:T(1,128)S(1)} %bitcast.172), channel_id=4, replica_groups=mesh['tm'=32,'frac'=16] {'frac'}, dimensions={0}, use_global_device_ids=true | all-gather | bytes 17408 | tf_op jit(solution)/shard_map/all_gather | solution.py:84
  238.9 6.1 gather_fusion.5
  245.0 5.9 scatter_custom_fusion.3
  254.8 15.2 %all-gather.11 = f32[16,1,256]{2,1,0:T(1,128)S(1)} all-gather(f32[1,1,256]{2,1,0:T(1,128)S(1)} %bitcast.173), channel_id=5, replica_groups=mesh['tm'=32,'frac'=16] {'frac'}, dimensions={0}, use_global_device_ids=true | all-gather | bytes 17408 | tf_op jit(solution)/shard_map/all_gather | solution.py:84
  270.0 6.1 gather_fusion.7
  286.2 6.6 %all-to-all-start = ((f32[32,4,32,128]{3,2,1,0:T(8,128)}), f32[32,4,32,128]{3,2,1,0:T(8,128)S(1)}, u32[]{:S(2)}, u32[]{:S(2)}) async-start(f32[32,4,32,128]{3,2,1,0:T(8,128)} %tile.4), calls=%async_computation | async-start | bytes 4194304 | tf_op jit(solution)/shard_map/all_to_all | solution.py:104
  292.8 49.9 %all-to-all-done = f32[32,4,32,128]{3,2,1,0:T(8,128)S(1)} async-done(((f32[32,4,32,128]{3,2,1,0:T(8,128)}), f32[32,4,32,128]{3,2,1,0:T(8,128)S(1)}, u32[]{:S(2)}, u32[]{:S(2)}) %all-to-all-start) | async-done | bytes 2097184 | tf_op jit(solution)/shard_map/all_to_all | solution.py:104
  342.7 51.1 %while.242 = (s32[]{:T(128)}, f32[4,32,128]{2,1,0:T(8,128)S(1)}, f32[4,32,128]{2,1,0:T(8,128)S(1)}, f32[4,32,128]{2,1,0:T(8,128)S(1)}, f32[4,32,128]{2,1,0:T(8,1...) while((s32[]{:T(128)}, f32[4,32,128]{2,1,0:T(8,128)S(1)}, ...), condition=%wide.region_22.23_spmd, body=%wide.region_19.22_spmd.sunk | while | flops 409125 | bytes 2921564 | solution.py:116
  395.6 15.4 %all-gather.12 = f32[16,1,256]{2,1,0:T(1,128)S(1)} all-gather(f32[1,1,256]{2,1,0:T(1,128)S(1)} %bitcast.174), channel_id=6, replica_groups=mesh['tm'=32,'frac'=16] {'frac'}, dimensions={0}, use_global_device_ids=true | all-gather | bytes 17408 | tf_op jit(solution)/shard_map/all_gather | solution.py:84
  411.1 6.1 gather_fusion.9
  426.9 15.2 %all-gather.13 = f32[16,1,256]{2,1,0:T(1,128)S(1)} all-gather(f32[1,1,256]{2,1,0:T(1,128)S(1)} %bitcast.175), channel_id=7, replica_groups=mesh['tm'=32,'frac'=16] {'frac'}, dimensions={0}, use_global_device_ids=true | all-gather | bytes 17408 | tf_op jit(solution)/shard_map/all_gather | solution.py:84
  442.2 6.1 gather_fusion.11
  458.1 15.1 %all-gather.14 = f32[16,1,256]{2,1,0:T(1,128)S(1)} all-gather(f32[1,1,256]{2,1,0:T(1,128)S(1)} %bitcast.176), channel_id=8, replica_groups=mesh['tm'=32,'frac'=16] {'frac'}, dimensions={0}, use_global_device_ids=true | all-gather | bytes 17408 | tf_op jit(solution)/shard_map/all_gather | solution.py:84
  473.2 6.1 gather_fusion.13
  489.0 15.2 %all-gather.15 = f32[16,1,256]{2,1,0:T(1,128)S(1)} all-gather(f32[1,1,256]{2,1,0:T(1,128)S(1)} %bitcast.169), channel_id=9, replica_groups=mesh['tm'=32,'frac'=16] {'frac'}, dimensions={0}, use_global_device_ids=true | all-gather | bytes 17408 | tf_op jit(solution)/shard_map/all_gather | solution.py:84
  504.3 6.1 gather_fusion.15
  526.2 49.9 %all-to-all-done.1 = f32[32,4,32,128]{3,2,1,0:T(8,128)S(1)} async-done(((f32[32,4,32,128]{3,2,1,0:T(8,128)}), f32[32,4,32,128]{3,2,1,0:T(8,128)S(1)}, u32[]{:S(2)}, u32[]{:S(2)}) %all-to-all-start.1) | async-done | bytes 2097184 | tf_op jit(solution)/shard_map/all_to_all | solution.py:104
  576.2 51.1 %while.249 = (s32[]{:T(128)}, f32[4,32,128]{2,1,0:T(8,128)S(1)}, f32[4,32,128]{2,1,0:T(8,128)S(1)}, f32[4,32,128]{2,1,0:T(8,128)S(1)}, f32[4,32,128]{2,1,0:T(8,1...) while((s32[]{:T(128)}, f32[4,32,128]{2,1,0:T(8,128)S(1)}, ...), condition=%wide.region_40.41_spmd, body=%wide.region_37.40_spmd.sunk | while | flops 409125 | bytes 2921564 | solution.py:116
  (1707 shorter events, 291.4 us)
Async XLA Ops:
  6.5 86.8 %all-gather.18.cloned.1.call-start = ((), (), s32[]{:S(2)}) async-start(), calls=%async_computation.2 | async-start | bytes 2162688 | tf_op jit(solution)/shard_map/all_gather | solution.py:96
  170.9 6.2 copy-start.5
  170.9 18.2 %copy-start = (f32[4,32,128]{2,1,0:T(8,128)S(1)}, f32[4,32,128]{2,1,0:T(8,128)}, u32[]{:S(2)}) copy-start(f32[4,32,128]{2,1,0:T(8,128)} %get-tuple-element.2571) | copy-start | bytes 196612
  170.9 18.2 %copy-start.2 = (f32[1,4,32,128]{3,2,1,0:T(8,128)S(1)}, f32[1,4,32,128]{3,2,1,0:T(8,128)}, u32[]{:S(2)}) copy-start(f32[1,4,32,128]{3,2,1,0:T(8,128)} %param.46) | copy-start | bytes 196612
  170.9 18.2 %copy-start.4 = (f32[4,32,128]{2,1,0:T(8,128)S(1)}, f32[4,32,128]{2,1,0:T(8,128)}, u32[]{:S(2)}) copy-start(f32[4,32,128]{2,1,0:T(8,128)} %param.45) | copy-start | bytes 196612
  207.9 12.1 %copy-start.1 = (f32[4,32,128]{2,1,0:T(8,128)S(1)}, f32[4,32,128]{2,1,0:T(8,128)}, u32[]{:S(2)}) copy-start(f32[4,32,128]{2,1,0:T(8,128)} %get-tuple-element.2577) | copy-start | bytes 196612
  286.2 56.5 %all-to-all-start = ((f32[32,4,32,128]{3,2,1,0:T(8,128)}), f32[32,4,32,128]{3,2,1,0:T(8,128)S(1)}, u32[]{:S(2)}, u32[]{:S(2)}) async-start(f32[32,4,32,128]{3,2,1,0:T(8,128)} %tile.4), calls=%async_computation | async-start | bytes 4194304 | tf_op jit(solution)/shard_map/all_to_all | solution.py:104
  520.5 55.7 %all-to-all-start.1 = ((f32[32,4,32,128]{3,2,1,0:T(8,128)}), f32[32,4,32,128]{3,2,1,0:T(8,128)S(1)}, u32[]{:S(2)}, u32[]{:S(2)}) async-start(f32[32,4,32,128]{3,2,1,0:T(8,128)} %tile.5), calls=%async_computation.1 | async-start | bytes 4194304 | tf_op jit(solution)/shard_map/all_to_all | solution.py:104
  627.3 0.6 copy-start.3
Sparse Core Ops, SparseCore 0:
  10.5 82.8 all-gather.17
